TPU v7x, 32 devices: a whole 2x2x4 slice. The times are simulated.
32 devices in a mesh: shard: 4 (over y, x), ctx: 2 (over core), tp: 4 (over z).
Axes of the slice: x: 2, y: 2, z: 4, core: 2. Of those that a mesh axis runs over, the one named last changes fastest.
Arguments:
- activations: bfloat16 [4, 2048, 1024], P('shard', 'ctx'), may hold values from -6 to 6
- timestep: int32 [4], P('shard'), may hold values from 0 to 999
- positions: int32 [4, 2048], P('shard', 'ctx'), may hold values from 0 to 16383
- qkv_weight: bfloat16 [3, 1024, 1024], P(None, 'shard', 'tp'), may hold values from -0.1875 to 0.1875
- out_weight: bfloat16 [1024, 1024], P('tp', 'shard'), may hold values from -4 to 4
- up_weight: bfloat16 [1024, 4096], P('shard', 'tp'), may hold values from -0.1875 to 0.1875
- down_weight: bfloat16 [4096, 1024], P('tp', 'shard'), may hold values from -0.125 to 0.125
- time_weight: bfloat16 [256, 4, 1024], P(None, None, 'shard'), may hold values from -0.1875 to 0.1875
- norm_gains: bfloat16 [2, 1024], P(None, 'shard'), may hold values from 0.5 to 1.5
- cotangent: bfloat16 [4, 2048, 1024], P('shard', 'ctx'), may hold values from -6 to 6
Outputs:
- output: bfloat16 [4, 2048, 1024], P('shard', 'ctx')
- input_grad: bfloat16 [4, 2048, 1024], P('shard', 'ctx')
- grad_qkv: float32 [3, 1024, 1024], P(None, 'shard', 'tp')
- grad_out: float32 [1024, 1024], P('tp', 'shard')
- grad_up: float32 [1024, 4096], P('shard', 'tp')
- grad_down: float32 [4096, 1024], P('tp', 'shard')
- grad_time: float32 [256, 4, 1024], P(None, None, 'shard')
- grad_gains: float32 [2, 1024], P(None, 'shard')
All inputs are finite; a program needn't handle non-finite values.
Results may differ from a plain program's by a relative error of at most 0.015.
Values may be sent and summed in bfloat16 or wider, within the bound.
No kernel may reach another device: no remote copies, remote signals or barrier semaphores. Data moves between devices by JAX's collectives and lax.ppermute only.
A program may use at most 320 MiB of HBM per device.

v0:
```python
from functools import partial
import math
import jax
import jax.numpy as jnp
from jax import lax
from jax.sharding import PartitionSpec as P

HEAD_DIM = 64
TEMB = 256
highest = lax.Precision.HIGHEST
norm_epsilon = 1e-05


def embed_time(timestep):
    half_width = TEMB // 2
    frequency = jnp.exp(-math.log(10000.0) * jnp.arange(half_width, dtype=jnp.float32) / half_width)
    angles = timestep.astype(jnp.float32)[:, None] * frequency[None, :]
    return jnp.concatenate([jnp.sin(angles), jnp.cos(angles)], axis=-1)


def rotary_tables(positions):
    half_width = HEAD_DIM // 2
    frequency = jnp.exp(-math.log(10000.0) * jnp.arange(half_width, dtype=jnp.float32) / half_width)
    angles = positions.astype(jnp.float32)[..., None] * frequency
    return (jnp.cos(angles), jnp.sin(angles))


def rotate(heads_in, cosines, sines):
    half_width = HEAD_DIM // 2
    first = heads_in[..., :half_width]
    second = heads_in[..., half_width:]
    cos_wide = cosines[..., None, :]
    sin_wide = sines[..., None, :]
    return jnp.concatenate(
        [first * cos_wide - second * sin_wide, second * cos_wide + first * sin_wide], axis=-1
    )


def unrotate(heads_in, cosines, sines):
    half_width = HEAD_DIM // 2
    first = heads_in[..., :half_width]
    second = heads_in[..., half_width:]
    cos_wide = cosines[..., None, :]
    sin_wide = sines[..., None, :]
    return jnp.concatenate(
        [first * cos_wide + second * sin_wide, second * cos_wide - first * sin_wide], axis=-1
    )


def scaled_norm(values, gain_vec, scaling, offset):
    centered = values - jnp.mean(values, axis=-1, keepdims=True)
    variance = jnp.mean(centered * centered, axis=-1, keepdims=True)
    inverse_std = lax.rsqrt(variance + norm_epsilon)
    normed = centered * inverse_std
    return (
        normed * gain_vec * (1.0 + scaling[:, None, :]) + offset[:, None, :],
        normed,
        inverse_std,
    )


def norm_back(grad_in, normed, inverse_std, gain_vec, scaling):
    factor = gain_vec * (1.0 + scaling[:, None, :])
    grad_normed = grad_in * factor
    grad_values = inverse_std * (
        grad_normed
        - jnp.mean(grad_normed, axis=-1, keepdims=True)
        - normed * jnp.mean(grad_normed * normed, axis=-1, keepdims=True)
    )
    grad_gain = jnp.sum(grad_in * normed * (1.0 + scaling[:, None, :]), axis=(0, 1))
    grad_scaling = jnp.sum(grad_in * normed * gain_vec, axis=1)
    grad_offset = jnp.sum(grad_in, axis=1)
    return (grad_values, grad_gain, grad_scaling, grad_offset)


def group_heads(field, per_group):
    seq_count, rows_count, _ = field.shape
    split = field.reshape(seq_count, rows_count, -1, HEAD_DIM).transpose(0, 2, 1, 3)
    return split.reshape(-1, per_group, rows_count, HEAD_DIM)


def ungroup_heads(field, seq_count):
    rows_count = field.shape[2]
    joined = field.reshape(seq_count, -1, rows_count, HEAD_DIM).transpose(0, 2, 1, 3)
    return joined.reshape(seq_count, rows_count, -1)


def attend_block(triple, scaling):
    queries, keys, values = triple
    scores = jnp.einsum("gqd,gkd->gqk", queries, keys, preferred_element_type=jnp.float32) * scaling
    top_score = jnp.max(scores, axis=-1, keepdims=True)
    raised = jnp.exp(scores - top_score)
    total = jnp.sum(raised, axis=-1, keepdims=True)
    weights = (raised / total).astype(jnp.bfloat16)
    attended = jnp.einsum("gqk,gkd->gqd", weights, values, preferred_element_type=jnp.float32)
    return (attended, (top_score + jnp.log(total))[..., 0])


def attend_back(bundle, scaling):
    queries, keys, values, grad_out, log_total = bundle
    scores = jnp.einsum("gqd,gkd->gqk", queries, keys, preferred_element_type=jnp.float32) * scaling
    weights = jnp.exp(scores - log_total[..., None])
    grad_values = jnp.einsum(
        "gqk,gqd->gkd", weights.astype(jnp.bfloat16), grad_out, preferred_element_type=jnp.float32
    )
    grad_weights = jnp.einsum("gqd,gkd->gqk", grad_out, values, preferred_element_type=jnp.float32)
    row_term = jnp.sum(weights * grad_weights, axis=-1, keepdims=True)
    grad_scores = (weights * (grad_weights - row_term)).astype(jnp.bfloat16)
    grad_queries = (
        jnp.einsum("gqk,gkd->gqd", grad_scores, keys, preferred_element_type=jnp.float32) * scaling
    )
    grad_keys = (
        jnp.einsum("gqk,gqd->gkd", grad_scores, queries, preferred_element_type=jnp.float32)
        * scaling
    )
    return (grad_queries, grad_keys, grad_values)


def gelu_slope(hidden):
    return (
        0.5 * (1.0 + lax.erf(hidden * 0.7071067811865476))
        + hidden * jnp.exp(-0.5 * hidden * hidden) * 0.3989422804014327
    )


def body(
    activations,
    timestep,
    positions,
    qkv_weight,
    out_weight,
    up_weight,
    down_weight,
    time_weight,
    norm_gains,
    cotangent,
):
    seq_count, tokens, width = activations.shape
    local_width = qkv_weight.shape[2]
    heads_local = local_width // HEAD_DIM
    per_group = min(heads_local, max(1, 512 // tokens))
    while heads_local % per_group:
        per_group -= 1
    scaling = HEAD_DIM ** (-0.5)
    full_qkv, full_out, full_up, full_down, full_time, full_gains = (
        lax.all_gather(qkv_weight, "shard", axis=1, tiled=True),
        lax.all_gather(out_weight, "shard", axis=1, tiled=True),
        lax.all_gather(up_weight, "shard", axis=0, tiled=True),
        lax.all_gather(down_weight, "shard", axis=1, tiled=True),
        lax.all_gather(time_weight, "shard", axis=2, tiled=True),
        lax.all_gather(norm_gains, "shard", axis=1, tiled=True),
    )
    gains_f = full_gains.astype(jnp.float32)
    embedding = embed_time(timestep)
    modulation = jnp.einsum(
        "sk,kcd->scd", embedding, full_time.astype(jnp.float32), precision=highest
    )
    cosines, sines = rotary_tables(positions)
    inputs_f = activations.astype(jnp.float32)
    first_out, normed_one, inverse_one = scaled_norm(
        inputs_f, gains_f[0], modulation[:, 0], modulation[:, 1]
    )
    first_low = first_out.astype(jnp.bfloat16)
    projected = jnp.einsum("std,cde->cste", first_low, full_qkv, preferred_element_type=jnp.float32)
    head_shape = (seq_count, tokens, heads_local, HEAD_DIM)
    query_rot = (
        rotate(projected[0].reshape(head_shape), cosines, sines)
        .reshape(seq_count, tokens, local_width)
        .astype(jnp.bfloat16)
    )
    key_rot = (
        rotate(projected[1].reshape(head_shape), cosines, sines)
        .reshape(seq_count, tokens, local_width)
        .astype(jnp.bfloat16)
    )
    value_low = projected[2].astype(jnp.bfloat16)
    keys_all, values_all = (
        lax.all_gather(key_rot, "ctx", axis=1, tiled=True),
        lax.all_gather(value_low, "ctx", axis=1, tiled=True),
    )
    query_groups = group_heads(query_rot, per_group)
    attended, log_total = lax.map(
        partial(attend_block, scaling=scaling),
        (query_groups, group_heads(keys_all, per_group), group_heads(values_all, per_group)),
    )
    attended_low = ungroup_heads(attended, seq_count).astype(jnp.bfloat16)
    branch_part = jnp.einsum(
        "ste,ed->std", attended_low, full_out, preferred_element_type=jnp.float32
    )
    middle = inputs_f + lax.psum(branch_part, "tp")
    second_out, normed_two, inverse_two = scaled_norm(
        middle, gains_f[1], modulation[:, 2], modulation[:, 3]
    )
    second_low = second_out.astype(jnp.bfloat16)
    hidden = jnp.einsum("std,df->stf", second_low, full_up, preferred_element_type=jnp.float32)
    activated = jax.nn.gelu(hidden, approximate=False).astype(jnp.bfloat16)
    mlp_part = jnp.einsum("stf,fd->std", activated, full_down, preferred_element_type=jnp.float32)
    output = (middle + lax.psum(mlp_part, "tp")).astype(jnp.bfloat16)
    back_qkv, back_out, back_up, back_down = (
        lax.all_gather(qkv_weight, "shard", axis=1, tiled=True),
        lax.all_gather(out_weight, "shard", axis=1, tiled=True),
        lax.all_gather(up_weight, "shard", axis=0, tiled=True),
        lax.all_gather(down_weight, "shard", axis=1, tiled=True),
    )
    keys_back, values_back = (
        lax.all_gather(key_rot, "ctx", axis=1, tiled=True),
        lax.all_gather(value_low, "ctx", axis=1, tiled=True),
    )
    grad_down = jnp.einsum("stf,std->fd", activated, cotangent, preferred_element_type=jnp.float32)
    grad_act = jnp.einsum("std,fd->stf", cotangent, back_down, preferred_element_type=jnp.float32)
    grad_hidden = (grad_act * gelu_slope(hidden)).astype(jnp.bfloat16)
    grad_up = jnp.einsum("std,stf->df", second_low, grad_hidden, preferred_element_type=jnp.float32)
    grad_second = lax.psum(
        jnp.einsum("stf,df->std", grad_hidden, back_up, preferred_element_type=jnp.float32), "tp"
    )
    grad_mid_norm, gain_two, scaling_two, offset_two = norm_back(
        grad_second, normed_two, inverse_two, gains_f[1], modulation[:, 2]
    )
    grad_middle = cotangent.astype(jnp.float32) + grad_mid_norm
    grad_branch = grad_middle.astype(jnp.bfloat16)
    grad_out = jnp.einsum(
        "ste,std->ed", attended_low, grad_branch, preferred_element_type=jnp.float32
    )
    grad_attended = jnp.einsum(
        "std,ed->ste", grad_branch, back_out, preferred_element_type=jnp.float32
    ).astype(jnp.bfloat16)
    grad_query_g, grad_key_g, grad_value_g = lax.map(
        partial(attend_back, scaling=scaling),
        (
            query_groups,
            group_heads(keys_back, per_group),
            group_heads(values_back, per_group),
            group_heads(grad_attended, per_group),
            log_total,
        ),
    )
    grad_key_all = ungroup_heads(grad_key_g, seq_count)
    grad_value_all = ungroup_heads(grad_value_g, seq_count)
    grad_key, grad_value = (
        lax.psum_scatter(grad_key_all, "ctx", scatter_dimension=1, tiled=True),
        lax.psum_scatter(grad_value_all, "ctx", scatter_dimension=1, tiled=True),
    )
    grad_query = ungroup_heads(grad_query_g, seq_count)
    query_back = unrotate(grad_query.reshape(head_shape), cosines, sines).reshape(
        seq_count, tokens, local_width
    )
    key_back = unrotate(grad_key.reshape(head_shape), cosines, sines).reshape(
        seq_count, tokens, local_width
    )
    grad_projected = jnp.stack([query_back, key_back, grad_value], axis=0).astype(jnp.bfloat16)
    grad_qkv = jnp.einsum(
        "std,cste->cde", first_low, grad_projected, preferred_element_type=jnp.float32
    )
    grad_first = lax.psum(
        jnp.einsum("cste,cde->std", grad_projected, back_qkv, preferred_element_type=jnp.float32),
        "tp",
    )
    grad_in_norm, gain_one, scaling_one, offset_one = norm_back(
        grad_first, normed_one, inverse_one, gains_f[0], modulation[:, 0]
    )
    input_grad = (grad_middle + grad_in_norm).astype(jnp.bfloat16)
    grad_modulation = jnp.stack([scaling_one, offset_one, scaling_two, offset_two], axis=1)
    grad_time = jnp.einsum("sk,scd->kcd", embedding, grad_modulation, precision=highest)
    grad_gains = jnp.stack([gain_one, gain_two], axis=0)
    shares = (
        lax.psum_scatter(grad_qkv, "shard", scatter_dimension=1, tiled=True),
        lax.psum_scatter(grad_out, "shard", scatter_dimension=1, tiled=True),
        lax.psum_scatter(grad_up, "shard", scatter_dimension=0, tiled=True),
        lax.psum_scatter(grad_down, "shard", scatter_dimension=1, tiled=True),
        lax.psum_scatter(grad_time, "shard", scatter_dimension=2, tiled=True),
        lax.psum_scatter(grad_gains, "shard", scatter_dimension=1, tiled=True),
    )
    shares = lax.psum((shares[0], shares[1], shares[2], shares[3], shares[4], shares[5]), "ctx")
    return (output, input_grad, shares[0], shares[1], shares[2], shares[3], shares[4], shares[5])


def solution(mesh):
    placed = (
        P("shard", "ctx", None),
        P("shard"),
        P("shard", "ctx"),
        P(None, "shard", "tp"),
        P("tp", "shard"),
        P("shard", "tp"),
        P("tp", "shard"),
        P(None, None, "shard"),
        P(None, "shard"),
        P("shard", "ctx", None),
    )
    return jax.shard_map(
        body,
        mesh=mesh,
        in_specs=placed,
        out_specs=(
            P("shard", "ctx", None),
            P("shard", "ctx", None),
            P(None, "shard", "tp"),
            P("tp", "shard"),
            P("shard", "tp"),
            P("tp", "shard"),
            P(None, None, "shard"),
            P(None, "shard"),
        ),
        check_vma=False,
    )
```

profile of v0, /device:TPU:0, one launch (start us, length us, event | category | flops | bytes accessed | tf_op | source)
XLA Modules:
  0.0 1433.2 jit_solution(13286509616975945891)
XLA Ops:
  11.3 9.6 all_gather.30
  24.3 23.4 %all-gather.8.cloned.1.call-done = bf16[256,4,1024]{2,1,0:T(4,128)(2,1)} async-done(((bf16[256,4,256]{2,1,0:T(4,128)(2,1)}), bf16[256,4,1024]{2,1,0:T(4,128)(2,1)}) %all-gather.8.cloned.1.call-update) | async-done | bytes 2097168 | tf_op jit(solution)/shard_map/all_gather | solution.py:150
  51.8 29.2 %all-gather.10.cloned.1.call-done = bf16[3,1024,256]{1,2,0:T(8,128)(2,1)} async-done(((bf16[3,256,256]{1,2,0:T(8,128)(2,1)}), bf16[3,1024,256]{1,2,0:T(8,128)(2,1)}) %all-gather.10.cloned.1.call-update) | async-done | bytes 1572880 | tf_op jit(solution)/shard_map/all_gather | solution.py:146
  88.6 14.1 all_gather.35
  111.5 35.0 %while.28 = (s32[]{:T(128)}, bf16[4,1,1024,64]{2,3,1,0:T(8,128)(2,1)}, f32[4,1,1024]{2,1,0:T(1,128)S(1)}, bf16[4,1,1024,64]{3,2,1,0:T(8,128)(2,1)S(1)}, bf16[4,1...) while((s32[]{:T(128)}, bf16[4,1,1024,64]{2,3,1,0:T(8,128)(2,1)}, ...), condition=%wide.region_5.6_spmd.clone, body=%wide.region_2.5_spmd.sunk.clone | while | flops 555744256 | bytes 30976136 | solution.py:182
  151.9 153.9 %all-reduce.7.cloned.1.call-done = f32[1,1024,1024]{2,1,0:T(8,128)} async-done(((f32[1,1024,1024]{2,1,0:T(8,128)}), f32[1,1024,1024]{2,1,0:T(8,128)}) %all-reduce.7.cloned.1.call-update) | async-done | bytes 4194320 | tf_op jit(solution)/shard_map/psum | solution.py:190
  311.0 31.0 %all-gather.14.cloned.1.call-done = bf16[1024,1024]{1,0:T(8,128)(2,1)} async-done(((bf16[256,1024]{1,0:T(8,128)(2,1)}), bf16[1024,1024]{1,0:T(8,128)(2,1)}) %all-gather.14.cloned.1.call-update) | async-done | bytes 2097168 | tf_op jit(solution)/shard_map/all_gather | solution.py:148
  342.0 15.0 %fusion.66 = (bf16[1024,1024]{1,0:T(8,128)(2,1)}, f32[1024,1024]{1,0:T(8,128)}) fusion(bf16[1024,1024]{1,0:T(8,128)(2,1)} %all-gather.14.cloned.1.call-done, f32[1,1024,1024]{2,1,0:T(8,128)} %copy-done, f32[1024]{0:T(1024)S(1)} %bitcast.301, f32[1024]{0:T(1024)S(1)} %bitcast.283, f32[1024]{0:T(1024)S(1)} %bitcast.279, f32[1024]{0:T(1024)S(1)} %add_rsqrt_fusion, ...), kind=kOutput, calls=%fused_computation.77 | convolution fusion | flops 2221932544 | bytes 12603392 | tf_op jit(solution)/shard_map/std,df->stf/dot_general | solution.py:195
  356.9 22.2 %all-gather.16.cloned.1.call-done = bf16[1024,1024]{1,0:T(8,128)(2,1)} async-done(((bf16[1024,256]{1,0:T(8,128)(2,1)}), bf16[1024,1024]{1,0:T(8,128)(2,1)}) %all-gather.16.cloned.1.call-update) | async-done | bytes 2097168 | tf_op jit(solution)/shard_map/all_gather | solution.py:149
  391.3 154.9 %all-reduce.9.cloned.1.call-done = f32[1,1024,1024]{2,1,0:T(8,128)} async-done(((f32[1,1024,1024]{2,1,0:T(8,128)}), f32[1,1024,1024]{2,1,0:T(8,128)}) %all-reduce.9.cloned.1.call-update) | async-done | bytes 4194320 | tf_op jit(solution)/shard_map/psum | solution.py:213
  560.0 51.6 %while.29 = (s32[]{:T(128)}, f32[4,1,1024,64]{2,3,1,0:T(8,128)}, f32[4,1,2048,64]{2,3,1,0:T(8,128)}, f32[4,1,2048,64]{2,3,1,0:T(8,128)}, bf16[4,1,1024,64]{3,2,1...) while((s32[]{:T(128)}, f32[4,1,1024,64]{2,3,1,0:T(8,128)}, ...), condition=%wide.region_15.16_spmd.clone, body=%wide.region_13.15_spmd.sunk.clone | while | flops 1367538688 | bytes 68977792 | solution.py:227
  624.5 9.5 reduce-scatter.15.cloned.1.call-done
  641.2 292.3 %all-reduce.11.cloned.1.call-done = (f32[1,1024,1024]{2,1,0:T(8,128)}, f32[1,1024,1024]{2,1,0:T(8,128)}) async-done(((f32[1,1024,1024]{2,1,0:T(8,128)}, f32[1,1024,1024]{2,1,0:T(8,128)}), (f32[1,1024,1024]{2,1,0:T(8,128)}, f32[1,1024,1024]{2,1,0:T(8,128)})) %all-reduce.11.cloned.1.call-update) | async-done | bytes 8388624 | tf_op jit(solution)/shard_map/psum | solution.py:198
  940.3 64.8 %copy.59 = f32[256,4,1024]{1,0,2:T(8,128)} copy(f32[256,4,1024]{2,1,0:T(4,128)} %broadcast_multiply_fusion) | data formatting | bytes 8388608
  1005.1 110.5 %reshape.619 = f32[1024,1024]{1,0:T(8,128)} reshape(f32[1024,256,4]{2,1,0:T(8,128)} %bitcast.86) | data formatting | bytes 8388608
  1128.5 7.7 fusion.106
  1143.3 24.2 %reduce-scatter.25.cloned.1.call-done = f32[256,1024]{1,0:T(8,128)} async-done(((f32[1024,1024]{1,0:T(8,128)}), f32[256,1024]{1,0:T(8,128)}) %reduce-scatter.25.cloned.1.call-update) | async-done | bytes 1048592
  1167.5 36.8 %reshape.620 = f32[256,256,4]{2,1,0:T(8,128)} reshape(f32[256,1024]{1,0:T(8,128)} %reduce-scatter.25.cloned.1.call-done) | data formatting | bytes 2097152
  1204.3 21.0 %copy.60 = f32[256,4,256]{2,1,0:T(4,128)} copy(f32[256,4,256]{1,0,2:T(8,128)} %bitcast.252) | data formatting | bytes 2097152
  1225.3 29.1 %reduce-scatter.23.cloned.1.call-done = f32[1024,256]{1,0:T(8,128)} async-done(((f32[1024,1024]{1,0:T(8,128)}), f32[1024,256]{1,0:T(8,128)}) %reduce-scatter.23.cloned.1.call-update) | async-done | bytes 1048592 | tf_op jit(solution)/shard_map/reduce_scatter | solution.py:269
  1254.5 55.8 %reduce-scatter.21.cloned.1.call-done = f32[256,1024]{1,0:T(8,128)} async-done(((f32[1024,1024]{1,0:T(8,128)}), f32[256,1024]{1,0:T(8,128)}) %reduce-scatter.21.cloned.1.call-update) | async-done | bytes 1048592 | tf_op jit(solution)/shard_map/reduce_scatter | solution.py:268
  1310.3 46.8 %reduce-scatter.17.cloned.1.call-done = f32[3,256,256]{1,2,0:T(8,128)} async-done(((f32[3,1024,256]{1,2,0:T(8,128)}), f32[3,256,256]{1,2,0:T(8,128)}) %reduce-scatter.17.cloned.1.call-update) | async-done | bytes 786448 | tf_op jit(solution)/shard_map/reduce_scatter | solution.py:266
  1366.4 18.8 %reduce-scatter.27.cloned.1.call-done = f32[256,2]{1,0:T(8,128)} async-done(((f32[1024,2]{1,0:T(8,128)}), f32[256,2]{1,0:T(8,128)}) %reduce-scatter.27.cloned.1.call-update) | async-done | bytes 2064
  1389.2 28.7 %all-reduce.13.cloned.1.call-done = (f32[3,256,256]{1,2,0:T(8,128)}, f32[256,256]{1,0:T(8,128)}, f32[256,1024]{1,0:T(8,128)}, f32[1024,256]{1,0:T(8,128)}, f32[256,4,256]{2,1,0:T(4,128)}) async-done(((f32[3,256,256]{1,2,0:T(8,128)}, f32[256,256]{1,0:T(8,128)}, f32[256,1024]{1,0:T(8,128)}, f32[1024,256]{1,0:T(8,128)}, f32[256,4,256]{2,1,0:T(4,128)}), (f32[3,256,256]{1,2,0:T(8,128)}, f32[256,256]{1,0:T(8,128)}, ...) | async-done | bytes 4194320 | tf_op jit(solution)/shard_map/psum | solution.py:273
  (286 shorter events, 217.9 us)
Async XLA Ops:
  7.2 40.6 %all-gather.8.cloned.1.call-start = ((), (), s32[]{:S(2)}) async-start(), calls=%async_computation.8 | async-start | bytes 2621440 | tf_op jit(solution)/shard_map/all_gather | solution.py:150
  7.9 73.1 %all-gather.10.cloned.1.call-start = ((), (), s32[]{:S(2)}) async-start(), calls=%async_computation.9 | async-start | bytes 1966080 | tf_op jit(solution)/shard_map/all_gather | solution.py:146
  9.9 96.0 %all-gather.12.cloned.1.call-start = ((), (), s32[]{:S(2)}) async-start(), calls=%async_computation.10 | async-start | bytes 1572864 | tf_op jit(solution)/shard_map/all_gather | solution.py:178
  23.8 522.3 %copy-start.36 = (f32[1,1024]{1,0:T(1,128)}, f32[1,1024]{1,0:T(1,128)S(1)}, u32[]{:S(2)}) copy-start(f32[1,1024]{1,0:T(1,128)S(1)} %get-tuple-element.239) | copy-start | bytes 12292
  51.8 494.3 %copy-start.39 = (f32[1,1,1024]{2,1,0:T(1,128)}, f32[1,1,1024]{2,1,0:T(1,128)S(1)}, u32[]{:S(2)}) copy-start(f32[1,1,1024]{2,1,0:T(1,128)S(1)} %get-tuple-element.233) | copy-start | bytes 12292
  86.3 22.4 %all-gather.18.cloned.1.call-start = ((), (), s32[]{:S(2)}) async-start(), calls=%async_computation.21 | async-start | bytes 1572864 | tf_op jit(solution)/shard_map/all_gather | solution.py:179
  88.5 217.2 %all-reduce.7.cloned.1.call-start = ((), (), s32[]{:S(2)}) async-start(), calls=%async_computation.11 | async-start | bytes 8388608 | tf_op jit(solution)/shard_map/psum | solution.py:190
  150.5 191.5 %all-gather.14.cloned.1.call-start = ((), (), s32[]{:S(2)}) async-start(), calls=%async_computation.12 | async-start | bytes 2621440 | tf_op jit(solution)/shard_map/all_gather | solution.py:148
  151.1 228.0 %all-gather.16.cloned.1.call-start = ((), (), s32[]{:S(2)}) async-start(), calls=%async_computation.13 | async-start | bytes 2621440 | tf_op jit(solution)/shard_map/all_gather | solution.py:149
  151.8 394.3 %all-reduce.9.cloned.1.call-start = ((), (), s32[]{:S(2)}) async-start(), calls=%async_computation.14 | async-start | bytes 8388608 | tf_op jit(solution)/shard_map/psum | solution.py:213
  391.0 231.4 %reduce-scatter.13.cloned.1.call-start = ((), (), s32[]{:S(2)}) async-start(), calls=%async_computation.15 | async-start | bytes 3145728 | tf_op jit(solution)/shard_map/reduce_scatter | solution.py:240
  611.6 22.4 %reduce-scatter.15.cloned.1.call-start = ((), (), s32[]{:S(2)}) async-start(), calls=%async_computation.16 | async-start | bytes 3145728 | tf_op jit(solution)/shard_map/reduce_scatter | solution.py:241
  614.6 318.9 %all-reduce.11.cloned.1.call-start = ((), (), s32[]{:S(2)}) async-start(), calls=%async_computation.24 | async-start | bytes 16777216 | tf_op jit(solution)/shard_map/psum | solution.py:198
  640.5 292.9 %copy-start.5 = (bf16[1,1024,1024]{2,1,0:T(8,128)(2,1)S(1)}, bf16[1,1024,1024]{2,1,0:T(8,128)(2,1)}, u32[]{:S(2)}) copy-start(bf16[1,1024,1024]{2,1,0:T(8,128)(2,1)} %param.14) | copy-start | bytes 6291460
  640.5 292.9 %copy-start.30 = (f32[1024]{0:T(1024)S(1)}, f32[1024]{0:T(1024)}, u32[]{:S(2)}) copy-start(f32[1024]{0:T(1024)} %copy-done.29) | copy-start | bytes 12292
  640.5 292.9 %copy-start.34 = (f32[1024]{0:T(1024)S(1)}, f32[1024]{0:T(1024)}, u32[]{:S(2)}) copy-start(f32[1024]{0:T(1024)} %copy-done.33) | copy-start | bytes 12292
  640.5 292.9 %copy-start.35 = (f32[1,1,1024]{2,1,0:T(1,128)S(1)}, f32[1,1,1024]{2,1,0:T(1,128)}, u32[]{:S(2)}) copy-start(f32[1,1,1024]{2,1,0:T(1,128)} %get-tuple-element.231) | copy-start | bytes 12292
  640.6 526.9 %reduce-scatter.25.cloned.1.call-start = ((), (), s32[]{:S(2)}) async-start(), calls=%async_computation.22 | async-start | bytes 5242880
  1115.6 109.7 %reduce-scatter.19.cloned.1.call-start = ((), (), s32[]{:S(2)}) async-start(), calls=%async_computation.18 | async-start | bytes 1310720 | tf_op jit(solution)/shard_map/reduce_scatter | solution.py:267
  1120.5 134.0 %reduce-scatter.23.cloned.1.call-start = ((), (), s32[]{:S(2)}) async-start(), calls=%async_computation.20 | async-start | bytes 5242880 | tf_op jit(solution)/shard_map/reduce_scatter | solution.py:269
  1127.9 182.4 %reduce-scatter.21.cloned.1.call-start = ((), (), s32[]{:S(2)}) async-start(), calls=%async_computation.19 | async-start | bytes 5242880 | tf_op jit(solution)/shard_map/reduce_scatter | solution.py:268
  1136.3 220.8 %reduce-scatter.17.cloned.1.call-start = ((), (), s32[]{:S(2)}) async-start(), calls=%async_computation.17 | async-start | bytes 3932160 | tf_op jit(solution)/shard_map/reduce_scatter | solution.py:266
  1142.1 243.0 %reduce-scatter.27.cloned.1.call-start = ((), (), s32[]{:S(2)}) async-start(), calls=%async_computation.23 | async-start | bytes 655360
  1143.3 274.5 %all-reduce.13.cloned.1.call-start = ((), (), s32[]{:S(2)}) async-start(), calls=%async_computation.25 | async-start | bytes 8388608 | tf_op jit(solution)/shard_map/psum | solution.py:273
  (58 other events, 1990.5 us)
Sparse Core Ops, SparseCore 0:
  9.8 37.8 all-gather.7
  50.1 30.8 all-gather.9
  86.5 9.0 all-gather.11
  97.5 10.1 all-gather.17
  150.6 155.0 all-reduce.6
  307.6 34.3 all-gather.13
  343.9 35.1 all-gather.15
  391.1 154.9 all-reduce.8
  611.7 8.5 reduce-scatter.12
  623.1 10.8 reduce-scatter.14
  640.7 292.6 all-reduce.10
  1115.7 51.7 reduce-scatter.24
  1171.2 27.6 reduce-scatter.18
  1201.8 52.6 reduce-scatter.22
  1257.6 52.6 reduce-scatter.20
  1313.1 43.9 reduce-scatter.16
  1360.4 24.7 reduce-scatter.26
  1388.8 28.9 all-reduce.12
where the time goes:
time: 1440 us; the launch traced here: 1430 us
  waiting for transfers between devices  922 us (64%)
  local copies, waits for them, and re-layouts  273 us (19%)
  matrix products  141 us (10%)
  other arithmetic  53.4 us (4%)
  blocking collectives  26.7 us (2%)
  between operations  15.8 us (1%)
    psum x1, waiting for transfers between devices, body(): output = (middle + lax.psum(mlp_part, 'tp')).astype(jnp.bfloat16)  292 us
    unnamed x116, local copies, waits for them, and re-layouts  255 us
    psum x1, waiting for transfers between devices, body(): lax.psum(jnp.einsum('stf,df->std', grad_hidden, back_up, preferred_elemen...  155 us
    psum x1, waiting for transfers between devices, body(): middle = inputs_f + lax.psum(branch_part, 'tp')  154 us
    reduce_scatter x1, waiting for transfers between devices, body(): lax.psum_scatter(grad_up, 'shard', scatter_dimension=0, tiled=True)  55.8 us
    reduce_scatter x1, waiting for transfers between devices, body(): lax.psum_scatter(grad_qkv, 'shard', scatter_dimension=1, tiled=True)  46.8 us
    unnamed x20, waiting for transfers between devices  44.9 us
    all_gather x1, waiting for transfers between devices, body(): lax.all_gather(up_weight, 'shard', axis=0, tiled=True)  31 us
  transfers between devices with their start and end apart: 18, of which 14 were waited for; matrix products, arithmetic and copies ran while one was open for 10% of the time, Pallas kernels for 0%

commit v1 on v0

--- a/solution.py
+++ b/solution.py
@@ -145,7 +145,9 @@
     full_qkv, full_out, full_up, full_down, full_time, full_gains = (
         lax.all_gather(qkv_weight, "shard", axis=1, tiled=True),
         lax.all_gather(out_weight, "shard", axis=1, tiled=True),
-        lax.all_gather(up_weight, "shard", axis=0, tiled=True),
+        jnp.concatenate(
+            lax.all_to_all(jnp.stack([up_weight] * lax.axis_size("shard")), "shard", 0, 0), axis=0
+        ),
         lax.all_gather(down_weight, "shard", axis=1, tiled=True),
         lax.all_gather(time_weight, "shard", axis=2, tiled=True),
         lax.all_gather(norm_gains, "shard", axis=1, tiled=True),

time: 1440 us -> 1440 us (level)
    unnamed x116 -> x112, local copies, waits for them, and re-layouts: 255 us -> 253 us
  transfers between devices with their start and end apart: 18 -> 19, of which waited for: 14 -> 14; matrix products, arithmetic and copies ran while one was open for 10% -> 10% of each run, Pallas kernels for 0% -> 0%
where the time goes in v1:
time: 1440 us; the launch traced here: 1430 us
  waiting for transfers between devices  908 us (63%)
  local copies, waits for them, and re-layouts  274 us (19%)
  matrix products  144 us (10%)
  other arithmetic  53.4 us (4%)
  blocking collectives  26.7 us (2%)
  between operations  15.8 us (1%)
    psum x1, waiting for transfers between devices, body(): output = (middle + lax.psum(mlp_part, 'tp')).astype(jnp.bfloat16)  292 us
    unnamed x112, local copies, waits for them, and re-layouts  253 us
    psum x1, waiting for transfers between devices, body(): lax.psum(jnp.einsum('stf,df->std', grad_hidden, back_up, preferred_elemen...  155 us
    psum x1, waiting for transfers between devices, body(): middle = inputs_f + lax.psum(branch_part, 'tp')  147 us
    reduce_scatter x1, waiting for transfers between devices, body(): lax.psum_scatter(grad_up, 'shard', scatter_dimension=0, tiled=True)  55.8 us
    reduce_scatter x1, waiting for transfers between devices, body(): lax.psum_scatter(grad_qkv, 'shard', scatter_dimension=1, tiled=True)  46.8 us
    unnamed x20, waiting for transfers between devices  44.9 us
    all_gather x1, waiting for transfers between devices, body(): lax.all_gather(up_weight, 'shard', axis=0, tiled=True)  30.6 us
  transfers between devices with their start and end apart: 19, of which 14 were waited for; matrix products, arithmetic and copies ran while one was open for 10% of the time, Pallas kernels for 0%

profile of v1, /device:TPU:0, one launch (start us, length us, event | category | flops | bytes accessed | tf_op | source)
XLA Modules:
  0.0 1428.0 jit_solution(17315601764469859636)
XLA Ops:
  11.3 9.6 all_gather.29
  24.3 23.4 %all-gather.8.cloned.1.call-done = bf16[256,4,1024]{2,1,0:T(4,128)(2,1)} async-done(((bf16[256,4,256]{2,1,0:T(4,128)(2,1)}), bf16[256,4,1024]{2,1,0:T(4,128)(2,1)}) %all-gather.8.cloned.1.call-update) | async-done | bytes 2097168 | tf_op jit(solution)/shard_map/all_gather | solution.py:152
  51.8 29.2 %all-gather.10.cloned.1.call-done = bf16[3,1024,256]{1,2,0:T(8,128)(2,1)} async-done(((bf16[3,256,256]{1,2,0:T(8,128)(2,1)}), bf16[3,1024,256]{1,2,0:T(8,128)(2,1)}) %all-gather.10.cloned.1.call-update) | async-done | bytes 1572880 | tf_op jit(solution)/shard_map/all_gather | solution.py:146
  88.6 14.1 all_gather.34
  111.5 35.0 %while.28 = (s32[]{:T(128)}, bf16[4,1,1024,64]{2,3,1,0:T(8,128)(2,1)}, f32[4,1,1024]{2,1,0:T(1,128)S(1)}, bf16[4,1,1024,64]{3,2,1,0:T(8,128)(2,1)S(1)}, bf16[4,1...) while((s32[]{:T(128)}, bf16[4,1,1024,64]{2,3,1,0:T(8,128)(2,1)}, ...), condition=%wide.region_5.6_spmd.clone, body=%wide.region_2.5_spmd.sunk.clone | while | flops 555744256 | bytes 30976136 | solution.py:184
  159.2 146.6 %all-reduce.7.cloned.1.call-done = f32[1,1024,1024]{2,1,0:T(8,128)} async-done(((f32[1,1024,1024]{2,1,0:T(8,128)}), f32[1,1024,1024]{2,1,0:T(8,128)}) %all-reduce.7.cloned.1.call-update) | async-done | bytes 4194320 | tf_op jit(solution)/shard_map/psum | solution.py:192
  311.0 15.0 %fusion.66 = (bf16[1024,1024]{1,0:T(8,128)(2,1)}, f32[1024,1024]{1,0:T(8,128)}) fusion(bf16[1024,1024]{1,0:T(8,128)(2,1)} %bitcast.47, f32[1,1024,1024]{2,1,0:T(8,128)} %copy-done, f32[1024]{0:T(1024)S(1)} %bitcast.302, f32[1024]{0:T(1024)S(1)} %bitcast.284, f32[1024]{0:T(1024)S(1)} %bitcast.280, f32[1024]{0:T(1024)S(1)} %add_rsqrt_fusion, ...), kind=kOutput, calls=%fused_computation.77 | convolution fusion | flops 2221932544 | bytes 12603392 | tf_op jit(solution)/shard_map/std,df->stf/dot_general | solution.py:197
  326.0 15.8 %all-gather.14.cloned.1.call-done = bf16[1024,1024]{1,0:T(8,128)(2,1)} async-done(((bf16[1024,256]{1,0:T(8,128)(2,1)}), bf16[1024,1024]{1,0:T(8,128)(2,1)}) %all-gather.14.cloned.1.call-update) | async-done | bytes 2097168 | tf_op jit(solution)/shard_map/all_gather | solution.py:151
  348.5 30.6 %all-gather.16.cloned.1.call-done = bf16[1024,1024]{1,0:T(8,128)(2,1)} async-done(((bf16[256,1024]{1,0:T(8,128)(2,1)}), bf16[1024,1024]{1,0:T(8,128)(2,1)}) %all-gather.16.cloned.1.call-update) | async-done | bytes 2097168 | tf_op jit(solution)/shard_map/all_gather | solution.py:204
  386.1 154.8 %all-reduce.9.cloned.1.call-done = f32[1,1024,1024]{2,1,0:T(8,128)} async-done(((f32[1,1024,1024]{2,1,0:T(8,128)}), f32[1,1024,1024]{2,1,0:T(8,128)}) %all-reduce.9.cloned.1.call-update) | async-done | bytes 4194320 | tf_op jit(solution)/shard_map/psum | solution.py:215
  554.8 51.6 %while.29 = (s32[]{:T(128)}, f32[4,1,1024,64]{2,3,1,0:T(8,128)}, f32[4,1,2048,64]{2,3,1,0:T(8,128)}, f32[4,1,2048,64]{2,3,1,0:T(8,128)}, bf16[4,1,1024,64]{3,2,1...) while((s32[]{:T(128)}, f32[4,1,1024,64]{2,3,1,0:T(8,128)}, ...), condition=%wide.region_15.16_spmd.clone, body=%wide.region_13.15_spmd.sunk.clone | while | flops 1367538688 | bytes 68977792 | solution.py:229
  619.3 9.5 reduce-scatter.15.cloned.1.call-done
  636.0 292.3 %all-reduce.11.cloned.1.call-done = (f32[1,1024,1024]{2,1,0:T(8,128)}, f32[1,1024,1024]{2,1,0:T(8,128)}) async-done(((f32[1,1024,1024]{2,1,0:T(8,128)}, f32[1,1024,1024]{2,1,0:T(8,128)}), (f32[1,1024,1024]{2,1,0:T(8,128)}, f32[1,1024,1024]{2,1,0:T(8,128)})) %all-reduce.11.cloned.1.call-update) | async-done | bytes 8388624 | tf_op jit(solution)/shard_map/psum | solution.py:200
  935.1 64.8 %copy.59 = f32[256,4,1024]{1,0,2:T(8,128)} copy(f32[256,4,1024]{2,1,0:T(4,128)} %broadcast_multiply_fusion) | data formatting | bytes 8388608
  999.9 110.5 %reshape.625 = f32[1024,1024]{1,0:T(8,128)} reshape(f32[1024,256,4]{2,1,0:T(8,128)} %bitcast.87) | data formatting | bytes 8388608
  1123.3 7.7 fusion.106
  1138.1 24.2 %reduce-scatter.25.cloned.1.call-done = f32[256,1024]{1,0:T(8,128)} async-done(((f32[1024,1024]{1,0:T(8,128)}), f32[256,1024]{1,0:T(8,128)}) %reduce-scatter.25.cloned.1.call-update) | async-done | bytes 1048592
  1162.3 36.8 %reshape.626 = f32[256,256,4]{2,1,0:T(8,128)} reshape(f32[256,1024]{1,0:T(8,128)} %reduce-scatter.25.cloned.1.call-done) | data formatting | bytes 2097152
  1199.1 21.0 %copy.60 = f32[256,4,256]{2,1,0:T(4,128)} copy(f32[256,4,256]{1,0,2:T(8,128)} %bitcast.253) | data formatting | bytes 2097152
  1220.1 29.1 %reduce-scatter.23.cloned.1.call-done = f32[1024,256]{1,0:T(8,128)} async-done(((f32[1024,1024]{1,0:T(8,128)}), f32[1024,256]{1,0:T(8,128)}) %reduce-scatter.23.cloned.1.call-update) | async-done | bytes 1048592 | tf_op jit(solution)/shard_map/reduce_scatter | solution.py:271
  1249.3 55.8 %reduce-scatter.21.cloned.1.call-done = f32[256,1024]{1,0:T(8,128)} async-done(((f32[1024,1024]{1,0:T(8,128)}), f32[256,1024]{1,0:T(8,128)}) %reduce-scatter.21.cloned.1.call-update) | async-done | bytes 1048592 | tf_op jit(solution)/shard_map/reduce_scatter | solution.py:270
  1305.1 46.8 %reduce-scatter.17.cloned.1.call-done = f32[3,256,256]{1,2,0:T(8,128)} async-done(((f32[3,1024,256]{1,2,0:T(8,128)}), f32[3,256,256]{1,2,0:T(8,128)}) %reduce-scatter.17.cloned.1.call-update) | async-done | bytes 786448 | tf_op jit(solution)/shard_map/reduce_scatter | solution.py:268
  1361.2 18.8 %reduce-scatter.27.cloned.1.call-done = f32[256,2]{1,0:T(8,128)} async-done(((f32[1024,2]{1,0:T(8,128)}), f32[256,2]{1,0:T(8,128)}) %reduce-scatter.27.cloned.1.call-update) | async-done | bytes 2064
  1383.9 28.7 %all-reduce.13.cloned.1.call-done = (f32[3,256,256]{1,2,0:T(8,128)}, f32[256,256]{1,0:T(8,128)}, f32[256,1024]{1,0:T(8,128)}, f32[1024,256]{1,0:T(8,128)}, f32[256,4,256]{2,1,0:T(4,128)}) async-done(((f32[3,256,256]{1,2,0:T(8,128)}, f32[256,256]{1,0:T(8,128)}, f32[256,1024]{1,0:T(8,128)}, f32[1024,256]{1,0:T(8,128)}, f32[256,4,256]{2,1,0:T(4,128)}), (f32[3,256,256]{1,2,0:T(8,128)}, f32[256,256]{1,0:T(8,128)}, ...) | async-done | bytes 4194320 | tf_op jit(solution)/shard_map/psum | solution.py:275
  (285 shorter events, 226.8 us)
Async XLA Ops:
  7.2 40.6 %all-gather.8.cloned.1.call-start = ((), (), s32[]{:S(2)}) async-start(), calls=%async_computation.9 | async-start | bytes 2621440 | tf_op jit(solution)/shard_map/all_gather | solution.py:152
  7.9 73.1 %all-gather.10.cloned.1.call-start = ((), (), s32[]{:S(2)}) async-start(), calls=%async_computation.10 | async-start | bytes 1966080 | tf_op jit(solution)/shard_map/all_gather | solution.py:146
  9.9 96.0 %all-gather.12.cloned.1.call-start = ((), (), s32[]{:S(2)}) async-start(), calls=%async_computation.11 | async-start | bytes 1572864 | tf_op jit(solution)/shard_map/all_gather | solution.py:180
  23.8 517.1 %copy-start.36 = (f32[1,1024]{1,0:T(1,128)}, f32[1,1024]{1,0:T(1,128)S(1)}, u32[]{:S(2)}) copy-start(f32[1,1024]{1,0:T(1,128)S(1)} %get-tuple-element.239) | copy-start | bytes 12292
  51.8 489.1 %copy-start.39 = (f32[1,1,1024]{2,1,0:T(1,128)}, f32[1,1,1024]{2,1,0:T(1,128)S(1)}, u32[]{:S(2)}) copy-start(f32[1,1,1024]{2,1,0:T(1,128)S(1)} %get-tuple-element.233) | copy-start | bytes 12292
  86.3 22.4 %all-gather.18.cloned.1.call-start = ((), (), s32[]{:S(2)}) async-start(), calls=%async_computation.22 | async-start | bytes 1572864 | tf_op jit(solution)/shard_map/all_gather | solution.py:181
  88.5 217.2 %all-reduce.7.cloned.1.call-start = ((), (), s32[]{:S(2)}) async-start(), calls=%async_computation.12 | async-start | bytes 8388608 | tf_op jit(solution)/shard_map/psum | solution.py:192
  150.5 191.3 %all-gather.14.cloned.1.call-start = ((), (), s32[]{:S(2)}) async-start(), calls=%async_computation.13 | async-start | bytes 2621440 | tf_op jit(solution)/shard_map/all_gather | solution.py:151
  153.8 157.2 %all-to-all-start = ((bf16[4,256,1024]{2,1,0:T(8,128)(2,1)}), bf16[4,256,1024]{2,1,0:T(8,128)(2,1)}, u32[]{:S(2)}, u32[]{:S(2)}) async-start(bf16[4,256,1024]{2,1,0:T(8,128)(2,1)} %stack.39), calls=%async_computation | async-start | bytes 4194304 | tf_op jit(solution)/shard_map/all_to_all | solution.py:149
  158.4 220.8 %all-gather.16.cloned.1.call-start = ((), (), s32[]{:S(2)}) async-start(), calls=%async_computation.14 | async-start | bytes 2621440 | tf_op jit(solution)/shard_map/all_gather | solution.py:204
  159.1 381.8 %all-reduce.9.cloned.1.call-start = ((), (), s32[]{:S(2)}) async-start(), calls=%async_computation.15 | async-start | bytes 8388608 | tf_op jit(solution)/shard_map/psum | solution.py:215
  385.8 231.4 %reduce-scatter.13.cloned.1.call-start = ((), (), s32[]{:S(2)}) async-start(), calls=%async_computation.16 | async-start | bytes 3145728 | tf_op jit(solution)/shard_map/reduce_scatter | solution.py:242
  606.4 22.4 %reduce-scatter.15.cloned.1.call-start = ((), (), s32[]{:S(2)}) async-start(), calls=%async_computation.17 | async-start | bytes 3145728 | tf_op jit(solution)/shard_map/reduce_scatter | solution.py:243
  609.4 318.9 %all-reduce.11.cloned.1.call-start = ((), (), s32[]{:S(2)}) async-start(), calls=%async_computation.25 | async-start | bytes 16777216 | tf_op jit(solution)/shard_map/psum | solution.py:200
  635.3 292.9 %copy-start.5 = (bf16[1,1024,1024]{2,1,0:T(8,128)(2,1)S(1)}, bf16[1,1024,1024]{2,1,0:T(8,128)(2,1)}, u32[]{:S(2)}) copy-start(bf16[1,1024,1024]{2,1,0:T(8,128)(2,1)} %param.14) | copy-start | bytes 6291460
  635.3 292.9 %copy-start.30 = (f32[1024]{0:T(1024)S(1)}, f32[1024]{0:T(1024)}, u32[]{:S(2)}) copy-start(f32[1024]{0:T(1024)} %copy-done.29) | copy-start | bytes 12292
  635.3 292.9 %copy-start.34 = (f32[1024]{0:T(1024)S(1)}, f32[1024]{0:T(1024)}, u32[]{:S(2)}) copy-start(f32[1024]{0:T(1024)} %copy-done.33) | copy-start | bytes 12292
  635.4 526.9 %reduce-scatter.25.cloned.1.call-start = ((), (), s32[]{:S(2)}) async-start(), calls=%async_computation.23 | async-start | bytes 5242880
  1110.4 109.7 %reduce-scatter.19.cloned.1.call-start = ((), (), s32[]{:S(2)}) async-start(), calls=%async_computation.19 | async-start | bytes 1310720 | tf_op jit(solution)/shard_map/reduce_scatter | solution.py:269
  1115.3 134.0 %reduce-scatter.23.cloned.1.call-start = ((), (), s32[]{:S(2)}) async-start(), calls=%async_computation.21 | async-start | bytes 5242880 | tf_op jit(solution)/shard_map/reduce_scatter | solution.py:271
  1122.7 182.4 %reduce-scatter.21.cloned.1.call-start = ((), (), s32[]{:S(2)}) async-start(), calls=%async_computation.20 | async-start | bytes 5242880 | tf_op jit(solution)/shard_map/reduce_scatter | solution.py:270
  1131.1 220.8 %reduce-scatter.17.cloned.1.call-start = ((), (), s32[]{:S(2)}) async-start(), calls=%async_computation.18 | async-start | bytes 3932160 | tf_op jit(solution)/shard_map/reduce_scatter | solution.py:268
  1136.9 243.0 %reduce-scatter.27.cloned.1.call-start = ((), (), s32[]{:S(2)}) async-start(), calls=%async_computation.24 | async-start | bytes 655360
  1138.1 274.5 %all-reduce.13.cloned.1.call-start = ((), (), s32[]{:S(2)}) async-start(), calls=%async_computation.26 | async-start | bytes 8388608 | tf_op jit(solution)/shard_map/psum | solution.py:275
  (57 other events, 2226.9 us)
Sparse Core Ops, SparseCore 0:
  9.8 37.8 all-gather.7
  50.1 30.8 all-gather.9
  86.5 9.0 all-gather.11
  97.5 10.1 all-gather.17
  150.6 155.0 all-reduce.6
  307.6 34.1 all-gather.13
  343.8 35.3 all-gather.15
  385.9 154.9 all-reduce.8
  606.5 8.5 reduce-scatter.12
  617.9 10.8 reduce-scatter.14
  635.5 292.6 all-reduce.10
  1110.5 51.7 reduce-scatter.24
  1166.0 27.6 reduce-scatter.18
  1196.6 52.6 reduce-scatter.22
  1252.4 52.6 reduce-scatter.20
  1307.9 43.9 reduce-scatter.16
  1355.2 24.7 reduce-scatter.26
  1383.6 28.9 all-reduce.12
